TPU v7x, 32 devices: a whole 2x2x4 slice. The times are simulated.
32 devices in a mesh: videos: 2 (over y), tm: 8 (over z, x), tile: 2 (over core).
Axes of the slice: x: 2, y: 2, z: 4, core: 2. Of those that a mesh axis runs over, the one named last changes fastest.
Arguments:
- latents: bfloat16 [32, 8, 32, 384], P(('videos', 'tm'), None, 'tile'), parts along dimension 0, may hold values from -6 to 6, as said below
- frame_counts: int32 [16], P(('videos', 'tm')), parts along dimension 0, may hold values from 1 to 2, as said below
- owners: int32 [32], P('videos'), parts along dimension 0, may hold values from 0 to 1
- w_time: bfloat16 [3, 384, 768], replicated, may hold values from -0.1875 to 0.1875
- b_time: float32 [768], replicated, may hold values from -3 to 3
- w_up: bfloat16 [3, 3, 384, 192], replicated, may hold values from -0.109375 to 0.109375
- b_up: float32 [192], replicated, may hold values from -3 to 3
Outputs:
- decoded: bfloat16 [64, 16, 12288], P(('videos', 'tm'), None, 'tile'), parts along dimension 0
There are 2 independent parts, one for each index of `videos`. A program takes and returns all parts, laid end to end along the dimension named above; an argument that names none is the same for every part. Nothing has to cross between parts.
Inputs may be any that keep to these rules, and one draw needn't show every extreme that they name: `frame_counts`: every device has one or two valid frames; in every draw some device has two and some has one. `latents`: in every slot and row, stored columns 12 to 15 of tile 0 equal the first 4 stored columns of tile 1.
All inputs are finite; a program needn't handle non-finite values.
Results may differ from a plain program's by a relative error of at most 0.0047.
Values may be sent and summed in bfloat16 or wider, within the bound.
No kernel may reach another device: no remote copies, remote signals or barrier semaphores. Data moves between devices by JAX's collectives and lax.ppermute only.
A program may use at most 128 MiB of HBM per device.

v0:
```python
import jax
import jax.numpy as jnp
from jax import lax
from jax.experimental import pallas as pl
from jax.experimental.pallas import tpu as pltpu
from jax.sharding import PartitionSpec as P

OV = 4
F32 = jnp.float32
BF16 = jnp.bfloat16
VMEM = pl.BlockSpec(memory_space=pltpu.VMEM)
SMEM = pl.BlockSpec(memory_space=pltpu.SMEM)
HBM = pl.BlockSpec(memory_space=pltpu.HBM)
LEAVES = 4
ABSENT = 16384.0
PARAMS = pltpu.CompilerParams(vmem_limit_bytes=24 << 20)


def dot(a, b):
    return jnp.dot(a, b, preferred_element_type=F32)


def dot_t(a, b):
    return lax.dot_general(a, b, (((1,), (1,)), ((), ())), preferred_element_type=F32)


def cost(flops, moved):
    return pl.CostEstimate(flops=flops, bytes_accessed=moved, transcendentals=0)


def prepare_weights(w_up, wp):
    outc, chans = w_up.shape[2], w_up.shape[3]
    for pr, block, rows in ((1, 1, (2,)), (0, 1, (1, 2)), (1, 0, (0, 1)), (0, 0, (0,))):
        taps = []
        for col in range(3):
            tap = w_up[rows[0], col].astype(F32)
            for row in rows[1:]:
                tap = tap + w_up[row, col].astype(F32)
            taps.append(tap)
        for k, tap in enumerate((taps[1] + taps[2], taps[0] + taps[1], taps[0], taps[2])):
            wp[pr, pl.ds(k * outc, outc), pl.ds(block * chans, chans)] = tap.astype(BF16)


def turner(rows, cols):
    i = lax.broadcasted_iota(jnp.int32, (rows * cols, rows * cols), 0)
    k = lax.broadcasted_iota(jnp.int32, (rows * cols, rows * cols), 1)
    return jnp.where(k == (i % rows) * cols + i // rows, 1.0, 0.0).astype(BF16)


def picker(rows, cols, col):
    i = lax.broadcasted_iota(jnp.int32, (rows, rows * cols), 0)
    k = lax.broadcasted_iota(jnp.int32, (rows, rows * cols), 1)
    return jnp.where(k == i * cols + col, 1.0, 0.0).astype(BF16)


def fill_x(t, mine, x, rows, cols):
    chans = t.shape[1] // 2
    t = t.astype(BF16).astype(F32)
    row = lax.broadcasted_iota(jnp.int32, (rows, 2 * chans), 0)
    for col in range(cols + 1):
        one = t[col * rows : (col + 1) * rows]
        up = jnp.where(row == 0, 0.0, pltpu.roll(one, 1, 0))
        down = jnp.where(row == rows - 1, 0.0, pltpu.roll(one, rows - 1, 0))
        for v, shifted in enumerate((up, one, down)):
            lanes = pl.ds(v * chans, chans)
            column = jnp.concatenate([shifted[:, :chans], shifted[:, chans:]], 0)
            if col < cols:
                x[pl.ds((col + 1) * 2 * rows, 2 * rows), lanes] = column.astype(BF16)
            else:
                x[pl.ds(0, 2 * rows), lanes] = jnp.where(mine == 1, column, 0.0).astype(BF16)
                x[pl.ds((cols + 1) * 2 * rows, 2 * rows), lanes] = jnp.where(mine == 0, column, 0.0).astype(BF16)


def convolve(x, wp, b_up, keep, mine, wide, done, rows, cols, copies):
    chans2 = wp.shape[2]
    chans = chans2 // 2
    column = 2 * rows
    outc = wp.shape[1] // 4
    lanes = 2 * outc
    strip_from = jnp.where(mine == 0, cols - OV, 0)
    soft = 1.0 - 0.5 / (2 * OV)
    bias = b_up[...].reshape(1, -1)
    bias = jnp.concatenate([bias, bias], -1)
    before_half = lax.broadcasted_iota(jnp.int32, (column, 128), 1) < outc % 128
    for pr in range(2):
        z = dot_t(x[:, pl.ds(pr * chans, chans2)], wp[pr])
        for col in range(cols):
            scale_l = scale_r = 1.0
            if col in (0, cols - OV):
                scale_l = jnp.where(strip_from == col, soft, 1.0)
            if col in (OV - 1, cols - 1):
                scale_r = jnp.where(strip_from + OV - 1 == col, soft, 1.0)
            here = z[(col + 1) * column : (col + 2) * column, :lanes] + bias
            prev = z[col * column : (col + 1) * column, lanes:] * scale_l
            after = z[(col + 2) * column : (col + 3) * column, lanes:] * scale_r
            tiles = []
            for j in range(lanes // 128):
                span = slice(j * 128, (j + 1) * 128)
                if (j + 1) * 128 <= outc:
                    add = prev[:, span]
                elif j * 128 >= outc:
                    add = after[:, span]
                else:
                    add = jnp.where(before_half, prev[:, span], after[:, span])
                tiles.append(here[:, span] + add)
            for h in range(2):
                for j, tile in enumerate(tiles):
                    wide[h, col * lanes // 128 + j, pl.ds(pr, rows, stride=2), :] = tile[h * rows : (h + 1) * rows]
    keep = keep[...] > 0.5
    for col in range(cols):
        shared = col < OV or col >= cols - OV
        outside = (col < strip_from) | (col >= strip_from + OV)
        for h in range(2):
            for lane in range(col * lanes, (col + 1) * lanes, 128):
                block = wide[h, lane // 128]
                if shared:
                    block = jnp.where(keep | outside, block, 0.0)
                done[h, :, pl.ds(lane, 128)] = block.astype(BF16)
        if copies and (col + 1) % (cols // LEAVES) == 0:
            copies[col // (cols // LEAVES)].start()


def leave(done, out, sems):
    width = done.shape[2] // LEAVES
    spans = [pl.ds(k * width, width) for k in range(LEAVES)]
    return [
        pltpu.make_async_copy(done.at[:, :, span], out.at[:, :, span], sems.at[k])
        for k, span in enumerate(spans)
    ]


def load_kernel(owners_hbm, own_hbm, b_time_hbm, b_up_hbm, keep, own, b_time, b_up, owners, sems):
    pairs = [(owners_hbm, owners), (own_hbm, own), (b_time_hbm, b_time), (b_up_hbm, b_up)]
    loads = [pltpu.make_async_copy(source, target, sems.at[k]) for k, (source, target) in enumerate(pairs)]
    for load in loads:
        load.start()
    mine = lax.axis_index("tile")
    loads[0].wait()
    out_row = lax.broadcasted_iota(jnp.int32, keep.shape, 0)
    owner = jnp.zeros(keep.shape, jnp.int32)
    for r in range(keep.shape[0]):
        owner = jnp.where(out_row == r, owners[r], owner)
    keep[...] = jnp.where(owner == mine, 1.0, 0.0)
    for load in loads[1:]:
        load.wait()


def pack_kernel(counts, own, own_far, latest, before):
    slots, rows, cols, chans = own.shape
    pixels = rows * cols
    mine = lax.axis_index("tile")
    two = counts[0] >= 2
    turn = turner(rows, cols)
    pick = picker(rows, cols, jnp.where(mine == 0, OV, cols - OV - 1))
    first, second = own[0].reshape(pixels, chans), own[1].reshape(pixels, chans)
    first_far, second_far = own_far[0].reshape(pixels, chans), own_far[1].reshape(pixels, chans)
    latest[pl.ds(0, pixels), :] = dot(turn, jnp.where(two, second, first)).astype(BF16)
    latest[pl.ds(pixels, rows), :] = dot(pick, jnp.where(two, second_far, first_far)).astype(BF16)
    before[pl.ds(0, pixels), :] = jnp.where(two, dot(turn, first), ABSENT).astype(BF16)
    before[pl.ds(pixels, rows), :] = jnp.where(two, dot(pick, first_far), ABSENT).astype(BF16)


def local_kernel(counts, latest, before, w_time, b_time, w_up, t0, t1, wp, lhs):
    two = counts[0] >= 2
    lhs[...] = jnp.where(two, before[...], latest[...])
    prepare_weights(w_up, wp)
    bias = b_time[...].reshape(1, -1)
    t0[...] = bias + dot(lhs[...], w_time[2])

    @pl.when(two)
    def _():
        t1[...] = bias + dot(latest[...], w_time[2]) + dot(lhs[...], w_time[1])


def near_kernel(counts, before, keep, newer, w_time, b_up, t1, wp, done, lhs, x, wide):
    rows = keep.shape[0] // 2
    cols = newer.shape[0] // rows - 1
    mine = lax.axis_index("tile")
    lhs[...] = jnp.where(lax.axis_index("tm") == 0, jnp.zeros_like(newer), newer[...])
    valid = counts[0] >= 2

    @pl.when(valid)
    def _():
        t = t1[...] + dot(lhs[...], w_time[0])
        fill_x(t, mine, x, rows, cols)
        convolve(x, wp, b_up, keep, mine, wide, done, rows, cols, [])

    @pl.when(jnp.logical_not(valid))
    def _():
        done[...] = jnp.zeros_like(done)


def far_kernel(
    keep, newer, near_before, far, w_time, b_up, t0, wp, second,
    out, lhs, x, wide, done, sems,
):
    early = pltpu.make_async_copy(second, out.at[pl.ds(2, 2)], sems.at[LEAVES])
    early.start()
    rows = keep.shape[0] // 2
    cols = far.shape[0] // rows - 1
    mine = lax.axis_index("tile")
    place_tm = lax.axis_index("tm")
    chans = far.shape[1]
    nearer = near_before[...].astype(F32)
    further = jnp.where(place_tm >= 2, far[...].astype(F32), 0.0)
    older = jnp.where(nearer < 0.5 * ABSENT, nearer, further)
    lhs[:, pl.ds(0, chans)] = jnp.where(place_tm == 0, 0.0, older).astype(BF16)
    lhs[:, pl.ds(chans, chans)] = jnp.where(place_tm == 0, jnp.zeros_like(newer), newer[...])
    t = t0[...] + dot(lhs[...], w_time[pl.ds(0, 2)].reshape(2 * chans, 2 * chans))
    fill_x(t, mine, x, rows, cols)
    copies = leave(done, out.at[pl.ds(0, 2)], sems)
    convolve(x, wp, b_up, keep, mine, wide, done, rows, cols, copies)
    for copy in copies + [early]:
        copy.wait()


def per_device(latents, frame_counts, owners, w_time, b_time, w_up, b_up):
    slots, rows, cols, chans = latents.shape
    outc = w_up.shape[3]
    ring = lax.axis_size("tm")
    pixels, extra = rows * cols, 2 * rows
    lanes = 2 * cols * outc
    shape = jax.ShapeDtypeStruct

    def step(k):
        return [(i, (i + k) % ring) for i in range(ring)]

    def stay(v):
        return pltpu.with_memory_space_constraint(v, pltpu.HBM)

    w_up = w_up.transpose(0, 1, 3, 2)
    own_far = lax.ppermute(latents, "tile", [(0, 1), (1, 0)])
    keep, own, b_time, b_up = pl.pallas_call(
        load_kernel,
        out_shape=(
            shape((extra, 128), F32),
            shape(latents.shape, BF16),
            shape(b_time.shape, F32),
            shape(b_up.shape, F32),
        ),
        in_specs=[HBM] * 4,
        out_specs=(VMEM,) * 4,
        scratch_shapes=[pltpu.SMEM(owners.shape, jnp.int32), pltpu.SemaphoreType.DMA((4,))],
        compiler_params=PARAMS,
        cost_estimate=cost(10**6, 1 << 10),
        name="load",
    )(stay(owners), stay(latents), stay(b_time), stay(b_up))
    frame = shape((pixels + rows, chans), BF16)
    latest, before = pl.pallas_call(
        pack_kernel,
        out_shape=(frame, frame),
        in_specs=[SMEM, VMEM, VMEM],
        out_specs=(VMEM,) * 2,
        compiler_params=PARAMS,
        cost_estimate=cost(3 * 10**9, 1 << 10),
        name="pack",
    )(frame_counts, own, own_far)
    newer = lax.ppermute(latest, "tm", step(1))
    far = lax.ppermute(latest, "tm", step(2))
    near_before = lax.ppermute(before, "tm", [(i, i + 1) for i in range(ring - 1)])
    partial = shape((pixels + rows, 2 * chans), F32)
    scratch = [
        pltpu.VMEM((pixels + rows, 2 * chans), BF16),
        pltpu.VMEM(((cols + 2) * extra, 3 * chans), BF16),
        pltpu.VMEM((2, lanes // 128, extra, 128), F32),
        pltpu.VMEM((2, extra, lanes), BF16),
        pltpu.SemaphoreType.DMA((LEAVES + 1,)),
    ]
    t0, t1, wp = pl.pallas_call(
        local_kernel,
        out_shape=(
            partial,
            partial,
            shape((2, 4 * outc, 2 * chans), BF16),
        ),
        in_specs=[SMEM] + [VMEM] * 5,
        out_specs=(VMEM,) * 3,
        scratch_shapes=[pltpu.VMEM(frame.shape, BF16)],
        compiler_params=PARAMS,
        cost_estimate=cost(10**6, 1 << 10),
        name="local",
    )(frame_counts, latest, before, w_time, b_time, w_up)
    second = pl.pallas_call(
        near_kernel,
        out_shape=shape((2, 2 * rows, lanes), BF16),
        in_specs=[SMEM] + [VMEM] * 7,
        out_specs=VMEM,
        scratch_shapes=[pltpu.VMEM(frame.shape, BF16)] + scratch[1:3],
        compiler_params=PARAMS,
        cost_estimate=cost(10**9, 4 << 20),
        name="near",
    )(frame_counts, before, keep, newer, w_time, b_up, t1, wp)
    return pl.pallas_call(
        far_kernel,
        out_shape=shape((2 * slots, 2 * rows, lanes), BF16),
        in_specs=[VMEM] * 9,
        out_specs=HBM,
        scratch_shapes=scratch,
        compiler_params=PARAMS,
        cost_estimate=cost(10**9, 4 << 20),
        name="far",
    )(keep, newer, near_before, far, w_time, b_up, t0, wp, second)


def solution(mesh):
    placed = (
        P(("videos", "tm"), None, "tile", None),
        P(("videos", "tm")),
        P("videos"),
        P(),
        P(),
        P(),
        P(),
    )
    return jax.shard_map(
        per_device,
        mesh=mesh,
        in_specs=placed,
        out_specs=P(("videos", "tm"), None, "tile"),
        check_vma=False,
    )
```

profile of v0, /device:TPU:24, one launch (start us, length us, event | category | flops | bytes accessed | tf_op | source)
XLA Modules:
  0.0 14.7 jit_solution(14822095834691235909)
XLA Ops:
  0.0 0.0 collective-permute-start
  0.7 1.0 %load.1 = (f32[16,128]{1,0:T(8,128)S(1)}, bf16[2,8,16,384]{3,2,1,0:T(8,128)(2,1)S(1)}, f32[768]{0:T(1024)S(1)}, f32[192]{0:T(256)S(1)}) custom-call(s32[16]{0:T(128)} %owners_hbm.1, bf16[2,8,16,384]{3,2,1,0:T(8,128)(2,1)} %own_hbm.1, f32[768]{0:T(1024)} %b_time_hbm.1, f32[192]{0:T(256)} %b_up_hbm.1), custom_call_target="tpu_custom_call" | custom-call | flops 1000000 | bytes 1024 | tf_op jit(solution)/shard_map/load/pallas_call | solution.py:233
  1.6 0.0 collective-permute-done.own_far
  1.7 0.0 copy-start
  1.7 0.0 copy-start.1
  1.7 0.2 %pack.1 = (bf16[136,384]{1,0:T(8,128)(2,1)S(1)}, bf16[136,384]{1,0:T(8,128)(2,1)S(1)}) custom-call(s32[1]{0:T(128)S(6)} %copy.8.counts, bf16[2,8,16,384]{3,2,1,0:T(8,128)(2,1)S(1)} %get-tuple-element.15.own, bf16[2,8,16,384]{3,2,1,0:T(8,128)(2,1)S(1)} %collective-permute-done.own_far), custom_call_target="tpu_custom_call" | custom-call | flops 3000000000 | bytes 1024 | tf_op jit(solution)/shard_map/pack/pallas_call | solution.py:249
  1.9 1.5 %collective-permute-start.1 = (bf16[136,384]{1,0:T(8,128)(2,1)S(1)}, bf16[136,384]{1,0:T(8,128)(2,1)S(1)}, u32[]{:S(2)}, u32[]{:S(2)}) collective-permute-start(bf16[136,384]{1,0:T(8,128)(2,1)S(1)} %get-tuple-element.16.latest), channel_id=1, source_target_pairs={{0,2},{2,4},{4,6},{6,8},{8,10},{10,12},{12,14},{14,0},{1,3},{3,5},... | collective-permute-start | bytes 313352 | tf_op jit(solution)/shard_map/ppermute | solution.py:258
  3.4 0.2 %collective-permute-start.3 = (bf16[136,384]{1,0:T(8,128)(2,1)S(1)}, bf16[136,384]{1,0:T(8,128)(2,1)S(1)}, u32[]{:S(2)}, u32[]{:S(2)}) collective-permute-start(bf16[136,384]{1,0:T(8,128)(2,1)S(1)} %get-tuple-element.16.latest), channel_id=1, source_target_pairs={{0,4},{2,6},{4,8},{6,10},{8,12},{10,14},{12,0},{14,2},{1,5},{3,7},... | collective-permute-start | bytes 313352 | tf_op jit(solution)/shard_map/ppermute | solution.py:259
  3.7 3.4 %collective-permute-start.2 = (bf16[136,384]{1,0:T(8,128)(2,1)S(1)}, bf16[136,384]{1,0:T(8,128)(2,1)S(1)}, u32[]{:S(2)}, u32[]{:S(2)}) collective-permute-start(bf16[136,384]{1,0:T(8,128)(2,1)S(1)} %get-tuple-element.17.before), channel_id=1, source_target_pairs={{0,2},{2,4},{4,6},{6,8},{8,10},{10,12},{12,14},{1,3},{3,5},{5,7},{... | collective-permute-start | bytes 313352 | tf_op jit(solution)/shard_map/ppermute | solution.py:260
  7.1 0.0 copy-done
  7.1 0.0 copy-done.1
  7.1 1.3 %local.1 = (f32[136,768]{1,0:T(8,128)S(1)}, f32[136,768]{1,0:T(8,128)S(1)}, bf16[2,768,768]{2,1,0:T(8,128)(2,1)S(1)}) custom-call(s32[1]{0:T(128)S(6)} %copy.8.counts, bf16[136,384]{1,0:T(8,128)(2,1)S(1)} %get-tuple-element.16.latest, bf16[136,384]{1,0:T(8,128)(2,1)S(1)} %get-tuple-element.17.before, bf16[3,384,768]{2,1,0:T(8,128)(2,1)S(1)} %copy-done, ...), custom_call_target="tpu_custom_call" | custom-call | flops 1000000 | bytes 1024 | tf_op jit(solution)/shard_map/local/pallas_call | solution.py:269
  8.5 0.1 collective-permute-done.1.newer
  8.6 1.2 %near.1.second = bf16[2,16,6144]{2,1,0:T(8,128)(2,1)S(1)} custom-call(s32[1]{0:T(128)S(6)} %copy.8.counts, bf16[136,384]{1,0:T(8,128)(2,1)S(1)} %get-tuple-element.17.before, f32[16,128]{1,0:T(8,128)S(1)} %get-tuple-element.14.keep, bf16[136,384]{1,0:T(8,128)(2,1)S(1)} %collective-permute-done.1.newer, bf16[3,384,768]{2,1,0:T(8,128)(2,1)S(1)} %copy-done, ...), custom_call_target="tpu_custom_call" | custom-call | flops 1000000000 | bytes 4194304 | tf_op jit(solution)/shard_map/near/pallas_call | solution.py:283
  9.8 0.0 collective-permute-done.3.far
  9.8 2.9 %collective-permute-done.2.near_before = bf16[136,384]{1,0:T(8,128)(2,1)S(1)} collective-permute-done((bf16[136,384]{1,0:T(8,128)(2,1)S(1)}, bf16[136,384]{1,0:T(8,128)(2,1)S(1)}, u32[]{:S(2)}, u32[]{:S(2)}) %collective-permute-start.2) | collective-permute-done | bytes 104480 | tf_op jit(solution)/shard_map/ppermute | solution.py:260
  12.7 2.1 %far.1 = bf16[4,16,6144]{2,1,0:T(8,128)(2,1)} custom-call(f32[16,128]{1,0:T(8,128)S(1)} %get-tuple-element.14.keep, bf16[136,384]{1,0:T(8,128)(2,1)S(1)} %collective-permute-done.1.newer, bf16[136,384]{1,0:T(8,128)(2,1)S(1)} %collective-permute-done.2.near_before, bf16[136,384]{1,0:T(8,128)(2,1)S(1)} %collective-permute-done.3.far, ...), custom_call_target="tpu_custom_call" | custom-call | flops 1000000000 | bytes 4194304 | tf_op jit(solution)/shard_map/far/pallas_call | solution.py:293
Async XLA Ops:
  0.0 1.7 %collective-permute-start = (bf16[2,8,16,384]{3,2,1,0:T(8,128)(2,1)}, bf16[2,8,16,384]{3,2,1,0:T(8,128)(2,1)S(1)}, u32[]{:S(2)}, u32[]{:S(2)}) collective-permute-start(bf16[2,8,16,384]{3,2,1,0:T(8,128)(2,1)} %own_hbm.1), channel_id=1, source_target_pairs={{0,1},{1,0},{2,3},{3,2},{4,5},{5,4},{6,7},{7,6},{8,9},{9,8},{10,11... | collective-permute-start | bytes 589832 | tf_op jit(solution)/shard_map/ppermute | solution.py:232
  1.7 5.5 %copy-start = (bf16[3,384,768]{2,1,0:T(8,128)(2,1)S(1)}, bf16[3,384,768]{2,1,0:T(8,128)(2,1)}, u32[]{:S(2)}) copy-start(bf16[3,384,768]{2,1,0:T(8,128)(2,1)} %w_time.5) | copy-start | bytes 5308420
  1.7 5.5 %copy-start.1 = (bf16[3,3,384,192]{2,3,1,0:T(8,128)(2,1)S(1)}, bf16[3,3,384,192]{2,3,1,0:T(8,128)(2,1)}, u32[]{:S(2)}) copy-start(bf16[3,3,384,192]{2,3,1,0:T(8,128)(2,1)} %param.12) | copy-start | bytes 3981316
  1.9 6.7 %collective-permute-start.1 = (bf16[136,384]{1,0:T(8,128)(2,1)S(1)}, bf16[136,384]{1,0:T(8,128)(2,1)S(1)}, u32[]{:S(2)}, u32[]{:S(2)}) collective-permute-start(bf16[136,384]{1,0:T(8,128)(2,1)S(1)} %get-tuple-element.16.latest), channel_id=1, source_target_pairs={{0,2},{2,4},{4,6},{6,8},{8,10},{10,12},{12,14},{14,0},{1,3},{3,5},... | collective-permute-start | bytes 313352 | tf_op jit(solution)/shard_map/ppermute | solution.py:258
  3.4 6.3 %collective-permute-start.3 = (bf16[136,384]{1,0:T(8,128)(2,1)S(1)}, bf16[136,384]{1,0:T(8,128)(2,1)S(1)}, u32[]{:S(2)}, u32[]{:S(2)}) collective-permute-start(bf16[136,384]{1,0:T(8,128)(2,1)S(1)} %get-tuple-element.16.latest), channel_id=1, source_target_pairs={{0,4},{2,6},{4,8},{6,10},{8,12},{10,14},{12,0},{14,2},{1,5},{3,7},... | collective-permute-start | bytes 313352 | tf_op jit(solution)/shard_map/ppermute | solution.py:259
  3.7 9.0 %collective-permute-start.2 = (bf16[136,384]{1,0:T(8,128)(2,1)S(1)}, bf16[136,384]{1,0:T(8,128)(2,1)S(1)}, u32[]{:S(2)}, u32[]{:S(2)}) collective-permute-start(bf16[136,384]{1,0:T(8,128)(2,1)S(1)} %get-tuple-element.17.before), channel_id=1, source_target_pairs={{0,2},{2,4},{4,6},{6,8},{8,10},{10,12},{12,14},{1,3},{3,5},{5,7},{... | collective-permute-start | bytes 313352 | tf_op jit(solution)/shard_map/ppermute | solution.py:260
where the time goes:
time: 14.9 us; the launch traced here: 14.7 us
  Pallas kernels  5.77 us (39%)
  starting transfers between devices  5.21 us (35%)
  waiting for transfers between devices  3 us (20%)
  between operations  0.73 us (5%)
    ppermute x1, starting transfers between devices, per_device(): lax.ppermute(before, 'tm', [(i, i + 1) for i in range(ring - 1)])  3.44 us
    ppermute x1, waiting for transfers between devices, per_device(): lax.ppermute(before, 'tm', [(i, i + 1) for i in range(ring - 1)])  2.88 us
    pallas_call x1, Pallas kernels, per_device(): pl.pallas_call(far_kernel, out_shape=shape((2 * slots, 2 * rows, lanes),...  2.06 us
    ppermute x1, starting transfers between devices, per_device(): newer = lax.ppermute(latest, 'tm', step(1))  1.54 us
    pallas_call x1, Pallas kernels, per_device(): pl.pallas_call(local_kernel, out_shape=(partial, partial, shape((2, 4 * o...  1.32 us
    pallas_call x1, Pallas kernels, per_device(): pl.pallas_call(near_kernel, out_shape=shape((2, 2 * rows, lanes), BF16),...  1.2 us
    pallas_call x1, Pallas kernels, per_device(): pl.pallas_call(load_kernel, out_shape=(shape((extra, 128), F32), shape(la...  0.97 us
  transfers between devices with their start and end apart: 4, of which 2 were waited for; matrix products, arithmetic and copies ran while one was open for 0% of the time, Pallas kernels for 24%

commit v1 on v0

--- a/solution.py
+++ b/solution.py
@@ -172,27 +172,39 @@
         t1[...] = bias + dot(latest[...], w_time[2]) + dot(lhs[...], w_time[1])
 
 
-def near_kernel(counts, before, keep, newer, w_time, b_up, t1, wp, done, lhs, x, wide):
+def add_halo(later, t, frame, weight, total):
+    @pl.when(later)
+    def _():
+        total[...] = t[...] + dot(frame[...], weight)
+
+    @pl.when(jnp.logical_not(later))
+    def _():
+        total[...] = t[...]
+
+
+def near_kernel(counts, before, keep, newer, w_time, b_up, t0, t1, wp, done, t0_new, total, x, wide):
     rows = keep.shape[0] // 2
     cols = newer.shape[0] // rows - 1
     mine = lax.axis_index("tile")
-    lhs[...] = jnp.where(lax.axis_index("tm") == 0, jnp.zeros_like(newer), newer[...])
+    later = lax.axis_index("tm") > 0
     valid = counts[0] >= 2
 
     @pl.when(valid)
     def _():
-        t = t1[...] + dot(lhs[...], w_time[0])
-        fill_x(t, mine, x, rows, cols)
+        add_halo(later, t1, newer, w_time[0], total)
+        fill_x(total[...], mine, x, rows, cols)
         convolve(x, wp, b_up, keep, mine, wide, done, rows, cols, [])
 
     @pl.when(jnp.logical_not(valid))
     def _():
         done[...] = jnp.zeros_like(done)
 
+    add_halo(later, t0, newer, w_time[1], t0_new)
+
 
 def far_kernel(
-    keep, newer, near_before, far, w_time, b_up, t0, wp, second,
-    out, lhs, x, wide, done, sems,
+    keep, far, near_before, w_time, b_up, t0, wp, second,
+    out, lhs, total, x, wide, done, sems,
 ):
     early = pltpu.make_async_copy(second, out.at[pl.ds(2, 2)], sems.at[LEAVES])
     early.start()
@@ -200,14 +212,12 @@
     cols = far.shape[0] // rows - 1
     mine = lax.axis_index("tile")
     place_tm = lax.axis_index("tm")
-    chans = far.shape[1]
     nearer = near_before[...].astype(F32)
     further = jnp.where(place_tm >= 2, far[...].astype(F32), 0.0)
     older = jnp.where(nearer < 0.5 * ABSENT, nearer, further)
-    lhs[:, pl.ds(0, chans)] = jnp.where(place_tm == 0, 0.0, older).astype(BF16)
-    lhs[:, pl.ds(chans, chans)] = jnp.where(place_tm == 0, jnp.zeros_like(newer), newer[...])
-    t = t0[...] + dot(lhs[...], w_time[pl.ds(0, 2)].reshape(2 * chans, 2 * chans))
-    fill_x(t, mine, x, rows, cols)
+    lhs[...] = older.astype(BF16)
+    add_halo(place_tm > 0, t0, lhs, w_time[0], total)
+    fill_x(total[...], mine, x, rows, cols)
     copies = leave(done, out.at[pl.ds(0, 2)], sems)
     convolve(x, wp, b_up, keep, mine, wide, done, rows, cols, copies)
     for copy in copies + [early]:
@@ -260,7 +270,8 @@
     near_before = lax.ppermute(before, "tm", [(i, i + 1) for i in range(ring - 1)])
     partial = shape((pixels + rows, 2 * chans), F32)
     scratch = [
-        pltpu.VMEM((pixels + rows, 2 * chans), BF16),
+        pltpu.VMEM(frame.shape, BF16),
+        pltpu.VMEM(partial.shape, F32),
         pltpu.VMEM(((cols + 2) * extra, 3 * chans), BF16),
         pltpu.VMEM((2, lanes // 128, extra, 128), F32),
         pltpu.VMEM((2, extra, lanes), BF16),
@@ -280,26 +291,26 @@
         cost_estimate=cost(10**6, 1 << 10),
         name="local",
     )(frame_counts, latest, before, w_time, b_time, w_up)
-    second = pl.pallas_call(
+    second, t0 = pl.pallas_call(
         near_kernel,
-        out_shape=shape((2, 2 * rows, lanes), BF16),
-        in_specs=[SMEM] + [VMEM] * 7,
-        out_specs=VMEM,
-        scratch_shapes=[pltpu.VMEM(frame.shape, BF16)] + scratch[1:3],
+        out_shape=(shape((2, 2 * rows, lanes), BF16), partial),
+        in_specs=[SMEM] + [VMEM] * 8,
+        out_specs=(VMEM, VMEM),
+        scratch_shapes=[pltpu.VMEM(partial.shape, F32)] + scratch[2:4],
         compiler_params=PARAMS,
         cost_estimate=cost(10**9, 4 << 20),
         name="near",
-    )(frame_counts, before, keep, newer, w_time, b_up, t1, wp)
+    )(frame_counts, before, keep, newer, w_time, b_up, t0, t1, wp)
     return pl.pallas_call(
         far_kernel,
         out_shape=shape((2 * slots, 2 * rows, lanes), BF16),
-        in_specs=[VMEM] * 9,
+        in_specs=[VMEM] * 8,
         out_specs=HBM,
         scratch_shapes=scratch,
         compiler_params=PARAMS,
         cost_estimate=cost(10**9, 4 << 20),
         name="far",
-    )(keep, newer, near_before, far, w_time, b_up, t0, wp, second)
+    )(keep, far, near_before, w_time, b_up, t0, wp, second)
 
 
 def solution(mesh):

time: 14.9 us -> 14.9 us (level)
  waiting for transfers between devices: 3 us -> 2.59 us
  Pallas kernels: 5.77 us -> 6.15 us
    pallas_call x1, Pallas kernels: 1.2 us -> 1.61 us  [per_device(): pl.pallas_call(near_kernel, out_shape=(shape((2, 2 * rows, lanes), BF16),...]
    ppermute x1, waiting for transfers between devices: 2.88 us -> 2.46 us  [per_device(): lax.ppermute(before, 'tm', [(i, i + 1) for i in range(ring - 1)])]
  transfers between devices with their start and end apart: 4 -> 4, of which waited for: 2 -> 2; matrix products, arithmetic and copies ran while one was open for 0% -> 0% of each run, Pallas kernels for 24% -> 27%
where the time goes in v1:
time: 14.9 us; the launch traced here: 14.7 us
  Pallas kernels  6.15 us (41%)
  starting transfers between devices  5.21 us (35%)
  waiting for transfers between devices  2.59 us (17%)
  between operations  0.73 us (5%)
    ppermute x1, starting transfers between devices, per_device(): lax.ppermute(before, 'tm', [(i, i + 1) for i in range(ring - 1)])  3.44 us
    ppermute x1, waiting for transfers between devices, per_device(): lax.ppermute(before, 'tm', [(i, i + 1) for i in range(ring - 1)])  2.46 us
    pallas_call x1, Pallas kernels, per_device(): pl.pallas_call(far_kernel, out_shape=shape((2 * slots, 2 * rows, lanes),...  2.02 us
    pallas_call x1, Pallas kernels, per_device(): pl.pallas_call(near_kernel, out_shape=(shape((2, 2 * rows, lanes), BF16),...  1.61 us
    ppermute x1, starting transfers between devices, per_device(): newer = lax.ppermute(latest, 'tm', step(1))  1.54 us
    pallas_call x1, Pallas kernels, per_device(): pl.pallas_call(local_kernel, out_shape=(partial, partial, shape((2, 4 * o...  1.33 us
    pallas_call x1, Pallas kernels, per_device(): pl.pallas_call(load_kernel, out_shape=(shape((extra, 128), F32), shape(la...  0.97 us
  transfers between devices with their start and end apart: 4, of which 2 were waited for; matrix products, arithmetic and copies ran while one was open for 0% of the time, Pallas kernels for 27%

profile of v1, /device:TPU:24, one launch (start us, length us, event | category | flops | bytes accessed | tf_op | source)
XLA Modules:
  0.0 14.7 jit_solution(2791976631082704201)
XLA Ops:
  0.0 0.0 collective-permute-start
  0.7 1.0 %load.1 = (f32[16,128]{1,0:T(8,128)S(1)}, bf16[2,8,16,384]{3,2,1,0:T(8,128)(2,1)S(1)}, f32[768]{0:T(1024)S(1)}, f32[192]{0:T(256)S(1)}) custom-call(s32[16]{0:T(128)} %owners_hbm.1, bf16[2,8,16,384]{3,2,1,0:T(8,128)(2,1)} %own_hbm.1, f32[768]{0:T(1024)} %b_time_hbm.1, f32[192]{0:T(256)} %b_up_hbm.1), custom_call_target="tpu_custom_call" | custom-call | flops 1000000 | bytes 1024 | tf_op jit(solution)/shard_map/load/pallas_call | solution.py:243
  1.6 0.0 collective-permute-done.own_far
  1.7 0.0 copy-start
  1.7 0.0 copy-start.1
  1.7 0.2 %pack.1 = (bf16[136,384]{1,0:T(8,128)(2,1)S(1)}, bf16[136,384]{1,0:T(8,128)(2,1)S(1)}) custom-call(s32[1]{0:T(128)S(6)} %copy.8.counts, bf16[2,8,16,384]{3,2,1,0:T(8,128)(2,1)S(1)} %get-tuple-element.17.own, bf16[2,8,16,384]{3,2,1,0:T(8,128)(2,1)S(1)} %collective-permute-done.own_far), custom_call_target="tpu_custom_call" | custom-call | flops 3000000000 | bytes 1024 | tf_op jit(solution)/shard_map/pack/pallas_call | solution.py:259
  1.9 1.5 %collective-permute-start.3 = (bf16[136,384]{1,0:T(8,128)(2,1)S(1)}, bf16[136,384]{1,0:T(8,128)(2,1)S(1)}, u32[]{:S(2)}, u32[]{:S(2)}) collective-permute-start(bf16[136,384]{1,0:T(8,128)(2,1)S(1)} %get-tuple-element.18.latest), channel_id=1, source_target_pairs={{0,2},{2,4},{4,6},{6,8},{8,10},{10,12},{12,14},{14,0},{1,3},{3,5},... | collective-permute-start | bytes 313352 | tf_op jit(solution)/shard_map/ppermute | solution.py:268
  3.4 0.2 %collective-permute-start.1 = (bf16[136,384]{1,0:T(8,128)(2,1)S(1)}, bf16[136,384]{1,0:T(8,128)(2,1)S(1)}, u32[]{:S(2)}, u32[]{:S(2)}) collective-permute-start(bf16[136,384]{1,0:T(8,128)(2,1)S(1)} %get-tuple-element.18.latest), channel_id=1, source_target_pairs={{0,4},{2,6},{4,8},{6,10},{8,12},{10,14},{12,0},{14,2},{1,5},{3,7},... | collective-permute-start | bytes 313352 | tf_op jit(solution)/shard_map/ppermute | solution.py:269
  3.7 3.4 %collective-permute-start.2 = (bf16[136,384]{1,0:T(8,128)(2,1)S(1)}, bf16[136,384]{1,0:T(8,128)(2,1)S(1)}, u32[]{:S(2)}, u32[]{:S(2)}) collective-permute-start(bf16[136,384]{1,0:T(8,128)(2,1)S(1)} %get-tuple-element.19.before), channel_id=1, source_target_pairs={{0,2},{2,4},{4,6},{6,8},{8,10},{10,12},{12,14},{1,3},{3,5},{5,7},{... | collective-permute-start | bytes 313352 | tf_op jit(solution)/shard_map/ppermute | solution.py:270
  7.1 0.0 copy-done
  7.1 0.0 copy-done.1
  7.1 1.3 %local.1 = (f32[136,768]{1,0:T(8,128)S(1)}, f32[136,768]{1,0:T(8,128)S(1)}, bf16[2,768,768]{2,1,0:T(8,128)(2,1)S(1)}) custom-call(s32[1]{0:T(128)S(6)} %copy.8.counts, bf16[136,384]{1,0:T(8,128)(2,1)S(1)} %get-tuple-element.18.latest, bf16[136,384]{1,0:T(8,128)(2,1)S(1)} %get-tuple-element.19.before, bf16[3,384,768]{2,1,0:T(8,128)(2,1)S(1)} %copy-done, ...), custom_call_target="tpu_custom_call" | custom-call | flops 1000000 | bytes 1024 | tf_op jit(solution)/shard_map/local/pallas_call | solution.py:280
  8.5 0.1 collective-permute-done.3.newer
  8.6 1.6 %near.1 = (bf16[2,16,6144]{2,1,0:T(8,128)(2,1)S(1)}, f32[136,768]{1,0:T(8,128)S(1)}) custom-call(s32[1]{0:T(128)S(6)} %copy.8.counts, bf16[136,384]{1,0:T(8,128)(2,1)S(1)} %get-tuple-element.19.before, f32[16,128]{1,0:T(8,128)S(1)} %get-tuple-element.16.keep, bf16[136,384]{1,0:T(8,128)(2,1)S(1)} %collective-permute-done.3.newer, ...), custom_call_target="tpu_custom_call" | custom-call | flops 1000000000 | bytes 4194304 | tf_op jit(solution)/shard_map/near/pallas_call | solution.py:294
  10.2 0.0 collective-permute-done.1.far
  10.2 2.5 %collective-permute-done.2.near_before = bf16[136,384]{1,0:T(8,128)(2,1)S(1)} collective-permute-done((bf16[136,384]{1,0:T(8,128)(2,1)S(1)}, bf16[136,384]{1,0:T(8,128)(2,1)S(1)}, u32[]{:S(2)}, u32[]{:S(2)}) %collective-permute-start.2) | collective-permute-done | bytes 104480 | tf_op jit(solution)/shard_map/ppermute | solution.py:270
  12.7 2.0 %far.1 = bf16[4,16,6144]{2,1,0:T(8,128)(2,1)} custom-call(f32[16,128]{1,0:T(8,128)S(1)} %get-tuple-element.16.keep, bf16[136,384]{1,0:T(8,128)(2,1)S(1)} %collective-permute-done.1.far, bf16[136,384]{1,0:T(8,128)(2,1)S(1)} %collective-permute-done.2.near_before, bf16[3,384,768]{2,1,0:T(8,128)(2,1)S(1)} %copy-done, f32[192]{0:T(256)S(1)} %get-tuple-element.20.b_up, ...), custom_call_target="tpu_custom_call" | custom-call | flops 1000000000 | bytes 4194304 | tf_op jit(solution)/shard_map/far/pallas_call | solution.py:304
Async XLA Ops:
  0.0 1.7 %collective-permute-start = (bf16[2,8,16,384]{3,2,1,0:T(8,128)(2,1)}, bf16[2,8,16,384]{3,2,1,0:T(8,128)(2,1)S(1)}, u32[]{:S(2)}, u32[]{:S(2)}) collective-permute-start(bf16[2,8,16,384]{3,2,1,0:T(8,128)(2,1)} %own_hbm.1), channel_id=1, source_target_pairs={{0,1},{1,0},{2,3},{3,2},{4,5},{5,4},{6,7},{7,6},{8,9},{9,8},{10,11... | collective-permute-start | bytes 589832 | tf_op jit(solution)/shard_map/ppermute | solution.py:242
  1.7 5.5 %copy-start = (bf16[3,384,768]{2,1,0:T(8,128)(2,1)S(1)}, bf16[3,384,768]{2,1,0:T(8,128)(2,1)}, u32[]{:S(2)}) copy-start(bf16[3,384,768]{2,1,0:T(8,128)(2,1)} %w_time.5) | copy-start | bytes 5308420
  1.7 5.5 %copy-start.1 = (bf16[3,3,384,192]{2,3,1,0:T(8,128)(2,1)S(1)}, bf16[3,3,384,192]{2,3,1,0:T(8,128)(2,1)}, u32[]{:S(2)}) copy-start(bf16[3,3,384,192]{2,3,1,0:T(8,128)(2,1)} %param.12) | copy-start | bytes 3981316
  1.9 6.7 %collective-permute-start.3 = (bf16[136,384]{1,0:T(8,128)(2,1)S(1)}, bf16[136,384]{1,0:T(8,128)(2,1)S(1)}, u32[]{:S(2)}, u32[]{:S(2)}) collective-permute-start(bf16[136,384]{1,0:T(8,128)(2,1)S(1)} %get-tuple-element.18.latest), channel_id=1, source_target_pairs={{0,2},{2,4},{4,6},{6,8},{8,10},{10,12},{12,14},{14,0},{1,3},{3,5},... | collective-permute-start | bytes 313352 | tf_op jit(solution)/shard_map/ppermute | solution.py:268
  3.4 6.8 %collective-permute-start.1 = (bf16[136,384]{1,0:T(8,128)(2,1)S(1)}, bf16[136,384]{1,0:T(8,128)(2,1)S(1)}, u32[]{:S(2)}, u32[]{:S(2)}) collective-permute-start(bf16[136,384]{1,0:T(8,128)(2,1)S(1)} %get-tuple-element.18.latest), channel_id=1, source_target_pairs={{0,4},{2,6},{4,8},{6,10},{8,12},{10,14},{12,0},{14,2},{1,5},{3,7},... | collective-permute-start | bytes 313352 | tf_op jit(solution)/shard_map/ppermute | solution.py:269
  3.7 9.0 %collective-permute-start.2 = (bf16[136,384]{1,0:T(8,128)(2,1)S(1)}, bf16[136,384]{1,0:T(8,128)(2,1)S(1)}, u32[]{:S(2)}, u32[]{:S(2)}) collective-permute-start(bf16[136,384]{1,0:T(8,128)(2,1)S(1)} %get-tuple-element.19.before), channel_id=1, source_target_pairs={{0,2},{2,4},{4,6},{6,8},{8,10},{10,12},{12,14},{1,3},{3,5},{5,7},{... | collective-permute-start | bytes 313352 | tf_op jit(solution)/shard_map/ppermute | solution.py:270

commit v2 on v1

--- a/solution.py
+++ b/solution.py
@@ -38,7 +38,12 @@
                 tap = tap + w_up[row, col].astype(F32)
             taps.append(tap)
         for k, tap in enumerate((taps[1] + taps[2], taps[0] + taps[1], taps[0], taps[2])):
-            wp[pr, pl.ds(k * outc, outc), pl.ds(block * chans, chans)] = tap.astype(BF16)
+            start = k % 2 * outc
+            for row in range(0, outc, 64):
+                tile, inside = divmod(start + row, 128)
+                target = tile * 256 + k // 2 * 128 + inside
+                piece = tap[row : row + 64].astype(BF16)
+                wp[pr, pl.ds(target, 64), pl.ds(block * chans, chans)] = piece
 
 
 def turner(rows, cols):
@@ -82,29 +87,26 @@
     bias = b_up[...].reshape(1, -1)
     bias = jnp.concatenate([bias, bias], -1)
     before_half = lax.broadcasted_iota(jnp.int32, (column, 128), 1) < outc % 128
-    for pr in range(2):
-        z = dot_t(x[:, pl.ds(pr * chans, chans2)], wp[pr])
-        for col in range(cols):
-            scale_l = scale_r = 1.0
-            if col in (0, cols - OV):
-                scale_l = jnp.where(strip_from == col, soft, 1.0)
-            if col in (OV - 1, cols - 1):
-                scale_r = jnp.where(strip_from + OV - 1 == col, soft, 1.0)
-            here = z[(col + 1) * column : (col + 2) * column, :lanes] + bias
-            prev = z[col * column : (col + 1) * column, lanes:] * scale_l
-            after = z[(col + 2) * column : (col + 3) * column, lanes:] * scale_r
-            tiles = []
-            for j in range(lanes // 128):
-                span = slice(j * 128, (j + 1) * 128)
+    for j in range(lanes // 128):
+        for pr in range(2):
+            z = dot_t(x[:, pl.ds(pr * chans, chans2)], wp[pr, pl.ds(j * 256, 256), :])
+            for col in range(cols):
+                scale_l = scale_r = 1.0
+                if col in (0, cols - OV):
+                    scale_l = jnp.where(strip_from == col, soft, 1.0)
+                if col in (OV - 1, cols - 1):
+                    scale_r = jnp.where(strip_from + OV - 1 == col, soft, 1.0)
+                here = z[(col + 1) * column : (col + 2) * column, :128] + bias[:, j * 128 : (j + 1) * 128]
+                prev = z[col * column : (col + 1) * column, 128:] * scale_l
+                after = z[(col + 2) * column : (col + 3) * column, 128:] * scale_r
                 if (j + 1) * 128 <= outc:
-                    add = prev[:, span]
+                    add = prev
                 elif j * 128 >= outc:
-                    add = after[:, span]
+                    add = after
                 else:
-                    add = jnp.where(before_half, prev[:, span], after[:, span])
-                tiles.append(here[:, span] + add)
-            for h in range(2):
-                for j, tile in enumerate(tiles):
+                    add = jnp.where(before_half, prev, after)
+                tile = here + add
+                for h in range(2):
                     wide[h, col * lanes // 128 + j, pl.ds(pr, rows, stride=2), :] = tile[h * rows : (h + 1) * rows]
     keep = keep[...] > 0.5
     for col in range(cols):

time: 14.9 us -> 14.9 us (level)
  no operation moved by 1% of the time
where the time goes in v2:
time: 14.9 us; the launch traced here: 14.7 us
  Pallas kernels  6.18 us (41%)
  starting transfers between devices  5.21 us (35%)
  waiting for transfers between devices  2.56 us (17%)
  between operations  0.73 us (5%)
    ppermute x1, starting transfers between devices, per_device(): lax.ppermute(before, 'tm', [(i, i + 1) for i in range(ring - 1)])  3.44 us
    ppermute x1, waiting for transfers between devices, per_device(): lax.ppermute(before, 'tm', [(i, i + 1) for i in range(ring - 1)])  2.43 us
    pallas_call x1, Pallas kernels, per_device(): pl.pallas_call(far_kernel, out_shape=shape((2 * slots, 2 * rows, lanes),...  2.02 us
    pallas_call x1, Pallas kernels, per_device(): pl.pallas_call(near_kernel, out_shape=(shape((2, 2 * rows, lanes), BF16),...  1.64 us
    ppermute x1, starting transfers between devices, per_device(): newer = lax.ppermute(latest, 'tm', step(1))  1.54 us
    pallas_call x1, Pallas kernels, per_device(): pl.pallas_call(local_kernel, out_shape=(partial, partial, shape((2, 4 * o...  1.33 us
    pallas_call x1, Pallas kernels, per_device(): pl.pallas_call(load_kernel, out_shape=(shape((extra, 128), F32), shape(la...  0.97 us
  transfers between devices with their start and end apart: 4, of which 2 were waited for; matrix products, arithmetic and copies ran while one was open for 0% of the time, Pallas kernels for 27%

profile of v2, /device:TPU:24, one launch (start us, length us, event | category | flops | bytes accessed | tf_op | source)
XLA Modules:
  0.0 14.7 jit_solution(10939403174710673704)
XLA Ops:
  0.0 0.0 collective-permute-start
  0.7 1.0 %load.1 = (f32[16,128]{1,0:T(8,128)S(1)}, bf16[2,8,16,384]{3,2,1,0:T(8,128)(2,1)S(1)}, f32[768]{0:T(1024)S(1)}, f32[192]{0:T(256)S(1)}) custom-call(s32[16]{0:T(128)} %owners_hbm.1, bf16[2,8,16,384]{3,2,1,0:T(8,128)(2,1)} %own_hbm.1, f32[768]{0:T(1024)} %b_time_hbm.1, f32[192]{0:T(256)} %b_up_hbm.1), custom_call_target="tpu_custom_call" | custom-call | flops 1000000 | bytes 1024 | tf_op jit(solution)/shard_map/load/pallas_call | solution.py:245
  1.6 0.0 collective-permute-done.own_far
  1.7 0.0 copy-start
  1.7 0.0 copy-start.1
  1.7 0.2 %pack.1 = (bf16[136,384]{1,0:T(8,128)(2,1)S(1)}, bf16[136,384]{1,0:T(8,128)(2,1)S(1)}) custom-call(s32[1]{0:T(128)S(6)} %copy.8.counts, bf16[2,8,16,384]{3,2,1,0:T(8,128)(2,1)S(1)} %get-tuple-element.17.own, bf16[2,8,16,384]{3,2,1,0:T(8,128)(2,1)S(1)} %collective-permute-done.own_far), custom_call_target="tpu_custom_call" | custom-call | flops 3000000000 | bytes 1024 | tf_op jit(solution)/shard_map/pack/pallas_call | solution.py:261
  1.9 1.5 %collective-permute-start.3 = (bf16[136,384]{1,0:T(8,128)(2,1)S(1)}, bf16[136,384]{1,0:T(8,128)(2,1)S(1)}, u32[]{:S(2)}, u32[]{:S(2)}) collective-permute-start(bf16[136,384]{1,0:T(8,128)(2,1)S(1)} %get-tuple-element.18.latest), channel_id=1, source_target_pairs={{0,2},{2,4},{4,6},{6,8},{8,10},{10,12},{12,14},{14,0},{1,3},{3,5},... | collective-permute-start | bytes 313352 | tf_op jit(solution)/shard_map/ppermute | solution.py:270
  3.4 0.2 %collective-permute-start.1 = (bf16[136,384]{1,0:T(8,128)(2,1)S(1)}, bf16[136,384]{1,0:T(8,128)(2,1)S(1)}, u32[]{:S(2)}, u32[]{:S(2)}) collective-permute-start(bf16[136,384]{1,0:T(8,128)(2,1)S(1)} %get-tuple-element.18.latest), channel_id=1, source_target_pairs={{0,4},{2,6},{4,8},{6,10},{8,12},{10,14},{12,0},{14,2},{1,5},{3,7},... | collective-permute-start | bytes 313352 | tf_op jit(solution)/shard_map/ppermute | solution.py:271
  3.7 3.4 %collective-permute-start.2 = (bf16[136,384]{1,0:T(8,128)(2,1)S(1)}, bf16[136,384]{1,0:T(8,128)(2,1)S(1)}, u32[]{:S(2)}, u32[]{:S(2)}) collective-permute-start(bf16[136,384]{1,0:T(8,128)(2,1)S(1)} %get-tuple-element.19.before), channel_id=1, source_target_pairs={{0,2},{2,4},{4,6},{6,8},{8,10},{10,12},{12,14},{1,3},{3,5},{5,7},{... | collective-permute-start | bytes 313352 | tf_op jit(solution)/shard_map/ppermute | solution.py:272
  7.1 0.0 copy-done
  7.1 0.0 copy-done.1
  7.1 1.3 %local.1 = (f32[136,768]{1,0:T(8,128)S(1)}, f32[136,768]{1,0:T(8,128)S(1)}, bf16[2,768,768]{2,1,0:T(8,128)(2,1)S(1)}) custom-call(s32[1]{0:T(128)S(6)} %copy.8.counts, bf16[136,384]{1,0:T(8,128)(2,1)S(1)} %get-tuple-element.18.latest, bf16[136,384]{1,0:T(8,128)(2,1)S(1)} %get-tuple-element.19.before, bf16[3,384,768]{2,1,0:T(8,128)(2,1)S(1)} %copy-done, ...), custom_call_target="tpu_custom_call" | custom-call | flops 1000000 | bytes 1024 | tf_op jit(solution)/shard_map/local/pallas_call | solution.py:282
  8.5 0.1 collective-permute-done.3.newer
  8.6 1.6 %near.1 = (bf16[2,16,6144]{2,1,0:T(8,128)(2,1)S(1)}, f32[136,768]{1,0:T(8,128)S(1)}) custom-call(s32[1]{0:T(128)S(6)} %copy.8.counts, bf16[136,384]{1,0:T(8,128)(2,1)S(1)} %get-tuple-element.19.before, f32[16,128]{1,0:T(8,128)S(1)} %get-tuple-element.16.keep, bf16[136,384]{1,0:T(8,128)(2,1)S(1)} %collective-permute-done.3.newer, ...), custom_call_target="tpu_custom_call" | custom-call | flops 1000000000 | bytes 4194304 | tf_op jit(solution)/shard_map/near/pallas_call | solution.py:296
  10.2 0.0 collective-permute-done.1.far
  10.2 2.4 %collective-permute-done.2.near_before = bf16[136,384]{1,0:T(8,128)(2,1)S(1)} collective-permute-done((bf16[136,384]{1,0:T(8,128)(2,1)S(1)}, bf16[136,384]{1,0:T(8,128)(2,1)S(1)}, u32[]{:S(2)}, u32[]{:S(2)}) %collective-permute-start.2) | collective-permute-done | bytes 104480 | tf_op jit(solution)/shard_map/ppermute | solution.py:272
  12.7 2.0 %far.1 = bf16[4,16,6144]{2,1,0:T(8,128)(2,1)} custom-call(f32[16,128]{1,0:T(8,128)S(1)} %get-tuple-element.16.keep, bf16[136,384]{1,0:T(8,128)(2,1)S(1)} %collective-permute-done.1.far, bf16[136,384]{1,0:T(8,128)(2,1)S(1)} %collective-permute-done.2.near_before, bf16[3,384,768]{2,1,0:T(8,128)(2,1)S(1)} %copy-done, f32[192]{0:T(256)S(1)} %get-tuple-element.20.b_up, ...), custom_call_target="tpu_custom_call" | custom-call | flops 1000000000 | bytes 4194304 | tf_op jit(solution)/shard_map/far/pallas_call | solution.py:306
Async XLA Ops:
  0.0 1.7 %collective-permute-start = (bf16[2,8,16,384]{3,2,1,0:T(8,128)(2,1)}, bf16[2,8,16,384]{3,2,1,0:T(8,128)(2,1)S(1)}, u32[]{:S(2)}, u32[]{:S(2)}) collective-permute-start(bf16[2,8,16,384]{3,2,1,0:T(8,128)(2,1)} %own_hbm.1), channel_id=1, source_target_pairs={{0,1},{1,0},{2,3},{3,2},{4,5},{5,4},{6,7},{7,6},{8,9},{9,8},{10,11... | collective-permute-start | bytes 589832 | tf_op jit(solution)/shard_map/ppermute | solution.py:244
  1.7 5.5 %copy-start = (bf16[3,384,768]{2,1,0:T(8,128)(2,1)S(1)}, bf16[3,384,768]{2,1,0:T(8,128)(2,1)}, u32[]{:S(2)}) copy-start(bf16[3,384,768]{2,1,0:T(8,128)(2,1)} %w_time.5) | copy-start | bytes 5308420
  1.7 5.5 %copy-start.1 = (bf16[3,3,384,192]{2,3,1,0:T(8,128)(2,1)S(1)}, bf16[3,3,384,192]{2,3,1,0:T(8,128)(2,1)}, u32[]{:S(2)}) copy-start(bf16[3,3,384,192]{2,3,1,0:T(8,128)(2,1)} %param.12) | copy-start | bytes 3981316
  1.9 6.7 %collective-permute-start.3 = (bf16[136,384]{1,0:T(8,128)(2,1)S(1)}, bf16[136,384]{1,0:T(8,128)(2,1)S(1)}, u32[]{:S(2)}, u32[]{:S(2)}) collective-permute-start(bf16[136,384]{1,0:T(8,128)(2,1)S(1)} %get-tuple-element.18.latest), channel_id=1, source_target_pairs={{0,2},{2,4},{4,6},{6,8},{8,10},{10,12},{12,14},{14,0},{1,3},{3,5},... | collective-permute-start | bytes 313352 | tf_op jit(solution)/shard_map/ppermute | solution.py:270
  3.4 6.8 %collective-permute-start.1 = (bf16[136,384]{1,0:T(8,128)(2,1)S(1)}, bf16[136,384]{1,0:T(8,128)(2,1)S(1)}, u32[]{:S(2)}, u32[]{:S(2)}) collective-permute-start(bf16[136,384]{1,0:T(8,128)(2,1)S(1)} %get-tuple-element.18.latest), channel_id=1, source_target_pairs={{0,4},{2,6},{4,8},{6,10},{8,12},{10,14},{12,0},{14,2},{1,5},{3,7},... | collective-permute-start | bytes 313352 | tf_op jit(solution)/shard_map/ppermute | solution.py:271
  3.7 9.0 %collective-permute-start.2 = (bf16[136,384]{1,0:T(8,128)(2,1)S(1)}, bf16[136,384]{1,0:T(8,128)(2,1)S(1)}, u32[]{:S(2)}, u32[]{:S(2)}) collective-permute-start(bf16[136,384]{1,0:T(8,128)(2,1)S(1)} %get-tuple-element.19.before), channel_id=1, source_target_pairs={{0,2},{2,4},{4,6},{6,8},{8,10},{10,12},{12,14},{1,3},{3,5},{5,7},{... | collective-permute-start | bytes 313352 | tf_op jit(solution)/shard_map/ppermute | solution.py:272

commit v3 on v2

--- a/solution.py
+++ b/solution.py
@@ -60,7 +60,6 @@
 
 def fill_x(t, mine, x, rows, cols):
     chans = t.shape[1] // 2
-    t = t.astype(BF16).astype(F32)
     row = lax.broadcasted_iota(jnp.int32, (rows, 2 * chans), 0)
     for col in range(cols + 1):
         one = t[col * rows : (col + 1) * rows]

time: 14.9 us -> 14.9 us (level)
  waiting for transfers between devices: 2.56 us -> 4.24 us
  Pallas kernels: 6.18 us -> 4.5 us
    ppermute x1, waiting for transfers between devices: 2.43 us -> 3.74 us  [per_device(): lax.ppermute(before, 'tm', [(i, i + 1) for i in range(ring - 1)])]
    pallas_call x1, Pallas kernels: 1.64 us -> 0.34 us  [per_device(): pl.pallas_call(near_kernel, out_shape=(shape((2, 2 * rows, lanes), BF16),...]
    pallas_call x1, Pallas kernels: 1.33 us -> 0.95 us  [per_device(): pl.pallas_call(local_kernel, out_shape=(partial, partial, shape((2, 4 * o...]
    ppermute x1, waiting for transfers between devices: 0.1 us -> 0.48 us  [per_device(): newer = lax.ppermute(latest, 'tm', step(1))]
  transfers between devices with their start and end apart: 4 -> 4, of which waited for: 2 -> 2; matrix products, arithmetic and copies ran while one was open for 0% -> 0% of each run, Pallas kernels for 27% -> 15%
where the time goes in v3:
time: 14.9 us; the launch traced here: 14.7 us
  starting transfers between devices  5.21 us (35%)
  Pallas kernels  4.5 us (30%)
  waiting for transfers between devices  4.24 us (28%)
  between operations  0.73 us (5%)
    ppermute x1, waiting for transfers between devices, per_device(): lax.ppermute(before, 'tm', [(i, i + 1) for i in range(ring - 1)])  3.74 us
    ppermute x1, starting transfers between devices, per_device(): lax.ppermute(before, 'tm', [(i, i + 1) for i in range(ring - 1)])  3.44 us
    pallas_call x1, Pallas kernels, per_device(): pl.pallas_call(far_kernel, out_shape=shape((2 * slots, 2 * rows, lanes),...  2.02 us
    ppermute x1, starting transfers between devices, per_device(): newer = lax.ppermute(latest, 'tm', step(1))  1.54 us
    pallas_call x1, Pallas kernels, per_device(): pl.pallas_call(load_kernel, out_shape=(shape((extra, 128), F32), shape(la...  0.97 us
    pallas_call x1, Pallas kernels, per_device(): pl.pallas_call(local_kernel, out_shape=(partial, partial, shape((2, 4 * o...  0.95 us
    ppermute x1, waiting for transfers between devices, per_device(): newer = lax.ppermute(latest, 'tm', step(1))  0.48 us
    pallas_call x1, Pallas kernels, per_device(): pl.pallas_call(near_kernel, out_shape=(shape((2, 2 * rows, lanes), BF16),...  0.34 us
  transfers between devices with their start and end apart: 4, of which 2 were waited for; matrix products, arithmetic and copies ran while one was open for 0% of the time, Pallas kernels for 15%

profile of v3, /device:TPU:24, one launch (start us, length us, event | category | flops | bytes accessed | tf_op | source)
XLA Modules:
  0.0 14.7 jit_solution(10939403174710673704)
XLA Ops:
  0.0 0.0 collective-permute-start
  0.7 1.0 %load.1 = (f32[16,128]{1,0:T(8,128)S(1)}, bf16[2,8,16,384]{3,2,1,0:T(8,128)(2,1)S(1)}, f32[768]{0:T(1024)S(1)}, f32[192]{0:T(256)S(1)}) custom-call(s32[16]{0:T(128)} %owners_hbm.1, bf16[2,8,16,384]{3,2,1,0:T(8,128)(2,1)} %own_hbm.1, f32[768]{0:T(1024)} %b_time_hbm.1, f32[192]{0:T(256)} %b_up_hbm.1), custom_call_target="tpu_custom_call" | custom-call | flops 1000000 | bytes 1024 | tf_op jit(solution)/shard_map/load/pallas_call | solution.py:244
  1.6 0.0 collective-permute-done.own_far
  1.7 0.0 copy-start
  1.7 0.0 copy-start.1
  1.7 0.2 %pack.1 = (bf16[136,384]{1,0:T(8,128)(2,1)S(1)}, bf16[136,384]{1,0:T(8,128)(2,1)S(1)}) custom-call(s32[1]{0:T(128)S(6)} %copy.8.counts, bf16[2,8,16,384]{3,2,1,0:T(8,128)(2,1)S(1)} %get-tuple-element.17.own, bf16[2,8,16,384]{3,2,1,0:T(8,128)(2,1)S(1)} %collective-permute-done.own_far), custom_call_target="tpu_custom_call" | custom-call | flops 3000000000 | bytes 1024 | tf_op jit(solution)/shard_map/pack/pallas_call | solution.py:260
  1.9 1.5 %collective-permute-start.3 = (bf16[136,384]{1,0:T(8,128)(2,1)S(1)}, bf16[136,384]{1,0:T(8,128)(2,1)S(1)}, u32[]{:S(2)}, u32[]{:S(2)}) collective-permute-start(bf16[136,384]{1,0:T(8,128)(2,1)S(1)} %get-tuple-element.18.latest), channel_id=1, source_target_pairs={{0,2},{2,4},{4,6},{6,8},{8,10},{10,12},{12,14},{14,0},{1,3},{3,5},... | collective-permute-start | bytes 313352 | tf_op jit(solution)/shard_map/ppermute | solution.py:269
  3.4 0.2 %collective-permute-start.1 = (bf16[136,384]{1,0:T(8,128)(2,1)S(1)}, bf16[136,384]{1,0:T(8,128)(2,1)S(1)}, u32[]{:S(2)}, u32[]{:S(2)}) collective-permute-start(bf16[136,384]{1,0:T(8,128)(2,1)S(1)} %get-tuple-element.18.latest), channel_id=1, source_target_pairs={{0,4},{2,6},{4,8},{6,10},{8,12},{10,14},{12,0},{14,2},{1,5},{3,7},... | collective-permute-start | bytes 313352 | tf_op jit(solution)/shard_map/ppermute | solution.py:270
  3.7 3.4 %collective-permute-start.2 = (bf16[136,384]{1,0:T(8,128)(2,1)S(1)}, bf16[136,384]{1,0:T(8,128)(2,1)S(1)}, u32[]{:S(2)}, u32[]{:S(2)}) collective-permute-start(bf16[136,384]{1,0:T(8,128)(2,1)S(1)} %get-tuple-element.19.before), channel_id=1, source_target_pairs={{0,2},{2,4},{4,6},{6,8},{8,10},{10,12},{12,14},{1,3},{3,5},{5,7},{... | collective-permute-start | bytes 313352 | tf_op jit(solution)/shard_map/ppermute | solution.py:271
  7.1 0.0 copy-done
  7.1 0.0 copy-done.1
  7.1 0.9 %local.1 = (f32[136,768]{1,0:T(8,128)S(1)}, f32[136,768]{1,0:T(8,128)S(1)}, bf16[2,768,768]{2,1,0:T(8,128)(2,1)S(1)}) custom-call(s32[1]{0:T(128)S(6)} %copy.8.counts, bf16[136,384]{1,0:T(8,128)(2,1)S(1)} %get-tuple-element.18.latest, bf16[136,384]{1,0:T(8,128)(2,1)S(1)} %get-tuple-element.19.before, bf16[3,384,768]{2,1,0:T(8,128)(2,1)S(1)} %copy-done, ...), custom_call_target="tpu_custom_call" | custom-call | flops 1000000 | bytes 1024 | tf_op jit(solution)/shard_map/local/pallas_call | solution.py:281
  8.1 0.5 %collective-permute-done.3.newer = bf16[136,384]{1,0:T(8,128)(2,1)S(1)} collective-permute-done((bf16[136,384]{1,0:T(8,128)(2,1)S(1)}, bf16[136,384]{1,0:T(8,128)(2,1)S(1)}, u32[]{:S(2)}, u32[]{:S(2)}) %collective-permute-start.3) | collective-permute-done | bytes 104480 | tf_op jit(solution)/shard_map/ppermute | solution.py:269
  8.6 0.3 %near.1 = (bf16[2,16,6144]{2,1,0:T(8,128)(2,1)S(1)}, f32[136,768]{1,0:T(8,128)S(1)}) custom-call(s32[1]{0:T(128)S(6)} %copy.8.counts, bf16[136,384]{1,0:T(8,128)(2,1)S(1)} %get-tuple-element.19.before, f32[16,128]{1,0:T(8,128)S(1)} %get-tuple-element.16.keep, bf16[136,384]{1,0:T(8,128)(2,1)S(1)} %collective-permute-done.3.newer, ...), custom_call_target="tpu_custom_call" | custom-call | flops 1000000000 | bytes 4194304 | tf_op jit(solution)/shard_map/near/pallas_call | solution.py:295
  8.9 0.0 collective-permute-done.1.far
  8.9 3.7 %collective-permute-done.2.near_before = bf16[136,384]{1,0:T(8,128)(2,1)S(1)} collective-permute-done((bf16[136,384]{1,0:T(8,128)(2,1)S(1)}, bf16[136,384]{1,0:T(8,128)(2,1)S(1)}, u32[]{:S(2)}, u32[]{:S(2)}) %collective-permute-start.2) | collective-permute-done | bytes 104480 | tf_op jit(solution)/shard_map/ppermute | solution.py:271
  12.7 2.0 %far.1 = bf16[4,16,6144]{2,1,0:T(8,128)(2,1)} custom-call(f32[16,128]{1,0:T(8,128)S(1)} %get-tuple-element.16.keep, bf16[136,384]{1,0:T(8,128)(2,1)S(1)} %collective-permute-done.1.far, bf16[136,384]{1,0:T(8,128)(2,1)S(1)} %collective-permute-done.2.near_before, bf16[3,384,768]{2,1,0:T(8,128)(2,1)S(1)} %copy-done, f32[192]{0:T(256)S(1)} %get-tuple-element.20.b_up, ...), custom_call_target="tpu_custom_call" | custom-call | flops 1000000000 | bytes 4194304 | tf_op jit(solution)/shard_map/far/pallas_call | solution.py:305
Async XLA Ops:
  0.0 1.7 %collective-permute-start = (bf16[2,8,16,384]{3,2,1,0:T(8,128)(2,1)}, bf16[2,8,16,384]{3,2,1,0:T(8,128)(2,1)S(1)}, u32[]{:S(2)}, u32[]{:S(2)}) collective-permute-start(bf16[2,8,16,384]{3,2,1,0:T(8,128)(2,1)} %own_hbm.1), channel_id=1, source_target_pairs={{0,1},{1,0},{2,3},{3,2},{4,5},{5,4},{6,7},{7,6},{8,9},{9,8},{10,11... | collective-permute-start | bytes 589832 | tf_op jit(solution)/shard_map/ppermute | solution.py:243
  1.7 5.5 %copy-start = (bf16[3,384,768]{2,1,0:T(8,128)(2,1)S(1)}, bf16[3,384,768]{2,1,0:T(8,128)(2,1)}, u32[]{:S(2)}) copy-start(bf16[3,384,768]{2,1,0:T(8,128)(2,1)} %w_time.5) | copy-start | bytes 5308420
  1.7 5.5 %copy-start.1 = (bf16[3,3,384,192]{2,3,1,0:T(8,128)(2,1)S(1)}, bf16[3,3,384,192]{2,3,1,0:T(8,128)(2,1)}, u32[]{:S(2)}) copy-start(bf16[3,3,384,192]{2,3,1,0:T(8,128)(2,1)} %param.12) | copy-start | bytes 3981316
  1.9 6.7 %collective-permute-start.3 = (bf16[136,384]{1,0:T(8,128)(2,1)S(1)}, bf16[136,384]{1,0:T(8,128)(2,1)S(1)}, u32[]{:S(2)}, u32[]{:S(2)}) collective-permute-start(bf16[136,384]{1,0:T(8,128)(2,1)S(1)} %get-tuple-element.18.latest), channel_id=1, source_target_pairs={{0,2},{2,4},{4,6},{6,8},{8,10},{10,12},{12,14},{14,0},{1,3},{3,5},... | collective-permute-start | bytes 313352 | tf_op jit(solution)/shard_map/ppermute | solution.py:269
  3.4 5.5 %collective-permute-start.1 = (bf16[136,384]{1,0:T(8,128)(2,1)S(1)}, bf16[136,384]{1,0:T(8,128)(2,1)S(1)}, u32[]{:S(2)}, u32[]{:S(2)}) collective-permute-start(bf16[136,384]{1,0:T(8,128)(2,1)S(1)} %get-tuple-element.18.latest), channel_id=1, source_target_pairs={{0,4},{2,6},{4,8},{6,10},{8,12},{10,14},{12,0},{14,2},{1,5},{3,7},... | collective-permute-start | bytes 313352 | tf_op jit(solution)/shard_map/ppermute | solution.py:270
  3.7 9.0 %collective-permute-start.2 = (bf16[136,384]{1,0:T(8,128)(2,1)S(1)}, bf16[136,384]{1,0:T(8,128)(2,1)S(1)}, u32[]{:S(2)}, u32[]{:S(2)}) collective-permute-start(bf16[136,384]{1,0:T(8,128)(2,1)S(1)} %get-tuple-element.19.before), channel_id=1, source_target_pairs={{0,2},{2,4},{4,6},{6,8},{8,10},{10,12},{12,14},{1,3},{3,5},{5,7},{... | collective-permute-start | bytes 313352 | tf_op jit(solution)/shard_map/ppermute | solution.py:271

commit v4 on v3

--- a/solution.py
+++ b/solution.py
@@ -11,7 +11,7 @@
 VMEM = pl.BlockSpec(memory_space=pltpu.VMEM)
 SMEM = pl.BlockSpec(memory_space=pltpu.SMEM)
 HBM = pl.BlockSpec(memory_space=pltpu.HBM)
-LEAVES = 4
+LEAVES = 2
 ABSENT = 16384.0
 PARAMS = pltpu.CompilerParams(vmem_limit_bytes=24 << 20)
 
@@ -213,10 +213,10 @@
     cols = far.shape[0] // rows - 1
     mine = lax.axis_index("tile")
     place_tm = lax.axis_index("tm")
-    nearer = near_before[...].astype(F32)
-    further = jnp.where(place_tm >= 2, far[...].astype(F32), 0.0)
-    older = jnp.where(nearer < 0.5 * ABSENT, nearer, further)
-    lhs[...] = older.astype(BF16)
+    nearer = near_before[...]
+    further = jnp.where(place_tm >= 2, far[...], jnp.zeros_like(far))
+    older = jnp.where(nearer < jnp.asarray(0.5 * ABSENT, BF16), nearer, further)
+    lhs[...] = older
     add_halo(place_tm > 0, t0, lhs, w_time[0], total)
     fill_x(total[...], mine, x, rows, cols)
     copies = leave(done, out.at[pl.ds(0, 2)], sems)

time: 14.9 us -> 14.9 us (level)
  the two profiles are of different devices: /device:TPU:24 before, /device:TPU:0 now
where the time goes in v4:
time: 14.9 us; the launch traced here: 14.7 us
  starting transfers between devices  8.02 us (54%)
  Pallas kernels  5.46 us (37%)
  between operations  0.75 us (5%)
  waiting for transfers between devices  0.43 us (3%)
    ppermute x1, starting transfers between devices, per_device(): lax.ppermute(before, 'tm', [(i, i + 1) for i in range(ring - 1)])  3.44 us
    ppermute x1, starting transfers between devices, per_device(): newer = lax.ppermute(latest, 'tm', step(1))  2.54 us
    pallas_call x1, Pallas kernels, per_device(): pl.pallas_call(far_kernel, out_shape=shape((2 * slots, 2 * rows, lanes),...  1.81 us
    ppermute x1, starting transfers between devices, per_device(): far = lax.ppermute(latest, 'tm', step(2))  1.58 us
    pallas_call x1, Pallas kernels, per_device(): pl.pallas_call(local_kernel, out_shape=(partial, partial, shape((2, 4 * o...  1.33 us
    pallas_call x1, Pallas kernels, per_device(): pl.pallas_call(near_kernel, out_shape=(shape((2, 2 * rows, lanes), BF16),...  1.13 us
    pallas_call x1, Pallas kernels, per_device(): pl.pallas_call(load_kernel, out_shape=(shape((extra, 128), F32), shape(la...  0.97 us
    ppermute x1, starting transfers between devices, per_device(): own_far = lax.ppermute(latents, 'tile', [(0, 1), (1, 0)])  0.45 us
  transfers between devices with their start and end apart: 4, of which 1 were waited for; matrix products, arithmetic and copies ran while one was open for 0% of the time, Pallas kernels for 23%

profile of v4, /device:TPU:0, one launch (start us, length us, event | category | flops | bytes accessed | tf_op | source)
XLA Modules:
  0.0 14.7 jit_solution(16178727176065494262)
XLA Ops:
  0.0 0.5 %collective-permute-start = (bf16[2,8,16,384]{3,2,1,0:T(8,128)(2,1)}, bf16[2,8,16,384]{3,2,1,0:T(8,128)(2,1)S(1)}, u32[]{:S(2)}, u32[]{:S(2)}) collective-permute-start(bf16[2,8,16,384]{3,2,1,0:T(8,128)(2,1)} %own_hbm.1), channel_id=1, source_target_pairs={{0,1},{1,0},{2,3},{3,2},{4,5},{5,4},{6,7},{7,6},{8,9},{9,8},{10,11... | collective-permute-start | bytes 589832 | tf_op jit(solution)/shard_map/ppermute | solution.py:243
  1.1 1.0 %load.1 = (f32[16,128]{1,0:T(8,128)S(1)}, bf16[2,8,16,384]{3,2,1,0:T(8,128)(2,1)S(1)}, f32[768]{0:T(1024)S(1)}, f32[192]{0:T(256)S(1)}) custom-call(s32[16]{0:T(128)} %owners_hbm.1, bf16[2,8,16,384]{3,2,1,0:T(8,128)(2,1)} %own_hbm.1, f32[768]{0:T(1024)} %b_time_hbm.1, f32[192]{0:T(256)} %b_up_hbm.1), custom_call_target="tpu_custom_call" | custom-call | flops 1000000 | bytes 1024 | tf_op jit(solution)/shard_map/load/pallas_call | solution.py:244
  2.1 0.0 collective-permute-done.own_far
  2.1 0.0 copy-start
  2.1 0.0 copy-start.1
  2.1 0.2 %pack.1 = (bf16[136,384]{1,0:T(8,128)(2,1)S(1)}, bf16[136,384]{1,0:T(8,128)(2,1)S(1)}) custom-call(s32[1]{0:T(128)S(6)} %copy.8.counts, bf16[2,8,16,384]{3,2,1,0:T(8,128)(2,1)S(1)} %get-tuple-element.17.own, bf16[2,8,16,384]{3,2,1,0:T(8,128)(2,1)S(1)} %collective-permute-done.own_far), custom_call_target="tpu_custom_call" | custom-call | flops 3000000000 | bytes 1024 | tf_op jit(solution)/shard_map/pack/pallas_call | solution.py:260
  2.3 2.5 %collective-permute-start.3 = (bf16[136,384]{1,0:T(8,128)(2,1)S(1)}, bf16[136,384]{1,0:T(8,128)(2,1)S(1)}, u32[]{:S(2)}, u32[]{:S(2)}) collective-permute-start(bf16[136,384]{1,0:T(8,128)(2,1)S(1)} %get-tuple-element.18.latest), channel_id=1, source_target_pairs={{0,2},{2,4},{4,6},{6,8},{8,10},{10,12},{12,14},{14,0},{1,3},{3,5},... | collective-permute-start | bytes 313352 | tf_op jit(solution)/shard_map/ppermute | solution.py:269
  4.9 1.6 %collective-permute-start.1 = (bf16[136,384]{1,0:T(8,128)(2,1)S(1)}, bf16[136,384]{1,0:T(8,128)(2,1)S(1)}, u32[]{:S(2)}, u32[]{:S(2)}) collective-permute-start(bf16[136,384]{1,0:T(8,128)(2,1)S(1)} %get-tuple-element.18.latest), channel_id=1, source_target_pairs={{0,4},{2,6},{4,8},{6,10},{8,12},{10,14},{12,0},{14,2},{1,5},{3,7},... | collective-permute-start | bytes 313352 | tf_op jit(solution)/shard_map/ppermute | solution.py:270
  6.5 3.4 %collective-permute-start.2 = (bf16[136,384]{1,0:T(8,128)(2,1)S(1)}, bf16[136,384]{1,0:T(8,128)(2,1)S(1)}, u32[]{:S(2)}, u32[]{:S(2)}) collective-permute-start(bf16[136,384]{1,0:T(8,128)(2,1)S(1)} %get-tuple-element.19.before), channel_id=1, source_target_pairs={{0,2},{2,4},{4,6},{6,8},{8,10},{10,12},{12,14},{1,3},{3,5},{5,7},{... | collective-permute-start | bytes 313352 | tf_op jit(solution)/shard_map/ppermute | solution.py:271
  9.9 0.0 copy-done
  9.9 0.0 copy-done.1
  9.9 1.3 %local.1 = (f32[136,768]{1,0:T(8,128)S(1)}, f32[136,768]{1,0:T(8,128)S(1)}, bf16[2,768,768]{2,1,0:T(8,128)(2,1)S(1)}) custom-call(s32[1]{0:T(128)S(6)} %copy.8.counts, bf16[136,384]{1,0:T(8,128)(2,1)S(1)} %get-tuple-element.18.latest, bf16[136,384]{1,0:T(8,128)(2,1)S(1)} %get-tuple-element.19.before, bf16[3,384,768]{2,1,0:T(8,128)(2,1)S(1)} %copy-done, ...), custom_call_target="tpu_custom_call" | custom-call | flops 1000000 | bytes 1024 | tf_op jit(solution)/shard_map/local/pallas_call | solution.py:281
  11.3 0.4 %collective-permute-done.3.newer = bf16[136,384]{1,0:T(8,128)(2,1)S(1)} collective-permute-done((bf16[136,384]{1,0:T(8,128)(2,1)S(1)}, bf16[136,384]{1,0:T(8,128)(2,1)S(1)}, u32[]{:S(2)}, u32[]{:S(2)}) %collective-permute-start.3) | collective-permute-done | bytes 104480 | tf_op jit(solution)/shard_map/ppermute | solution.py:269
  11.7 1.1 %near.1 = (bf16[2,16,6144]{2,1,0:T(8,128)(2,1)S(1)}, f32[136,768]{1,0:T(8,128)S(1)}) custom-call(s32[1]{0:T(128)S(6)} %copy.8.counts, bf16[136,384]{1,0:T(8,128)(2,1)S(1)} %get-tuple-element.19.before, f32[16,128]{1,0:T(8,128)S(1)} %get-tuple-element.16.keep, bf16[136,384]{1,0:T(8,128)(2,1)S(1)} %collective-permute-done.3.newer, ...), custom_call_target="tpu_custom_call" | custom-call | flops 1000000000 | bytes 4194304 | tf_op jit(solution)/shard_map/near/pallas_call | solution.py:295
  12.8 0.0 collective-permute-done.1.far
  12.9 0.0 collective-permute-done.2.near_before
  12.9 1.8 %far.1 = bf16[4,16,6144]{2,1,0:T(8,128)(2,1)} custom-call(f32[16,128]{1,0:T(8,128)S(1)} %get-tuple-element.16.keep, bf16[136,384]{1,0:T(8,128)(2,1)S(1)} %collective-permute-done.1.far, bf16[136,384]{1,0:T(8,128)(2,1)S(1)} %collective-permute-done.2.near_before, bf16[3,384,768]{2,1,0:T(8,128)(2,1)S(1)} %copy-done, f32[192]{0:T(256)S(1)} %get-tuple-element.20.b_up, ...), custom_call_target="tpu_custom_call" | custom-call | flops 1000000000 | bytes 4194304 | tf_op jit(solution)/shard_map/far/pallas_call | solution.py:305
Async XLA Ops:
  0.0 2.1 %collective-permute-start = (bf16[2,8,16,384]{3,2,1,0:T(8,128)(2,1)}, bf16[2,8,16,384]{3,2,1,0:T(8,128)(2,1)S(1)}, u32[]{:S(2)}, u32[]{:S(2)}) collective-permute-start(bf16[2,8,16,384]{3,2,1,0:T(8,128)(2,1)} %own_hbm.1), channel_id=1, source_target_pairs={{0,1},{1,0},{2,3},{3,2},{4,5},{5,4},{6,7},{7,6},{8,9},{9,8},{10,11... | collective-permute-start | bytes 589832 | tf_op jit(solution)/shard_map/ppermute | solution.py:243
  2.1 7.8 %copy-start = (bf16[3,384,768]{2,1,0:T(8,128)(2,1)S(1)}, bf16[3,384,768]{2,1,0:T(8,128)(2,1)}, u32[]{:S(2)}) copy-start(bf16[3,384,768]{2,1,0:T(8,128)(2,1)} %w_time.5) | copy-start | bytes 5308420
  2.1 7.8 %copy-start.1 = (bf16[3,3,384,192]{2,3,1,0:T(8,128)(2,1)S(1)}, bf16[3,3,384,192]{2,3,1,0:T(8,128)(2,1)}, u32[]{:S(2)}) copy-start(bf16[3,3,384,192]{2,3,1,0:T(8,128)(2,1)} %param.12) | copy-start | bytes 3981316
  2.3 9.4 %collective-permute-start.3 = (bf16[136,384]{1,0:T(8,128)(2,1)S(1)}, bf16[136,384]{1,0:T(8,128)(2,1)S(1)}, u32[]{:S(2)}, u32[]{:S(2)}) collective-permute-start(bf16[136,384]{1,0:T(8,128)(2,1)S(1)} %get-tuple-element.18.latest), channel_id=1, source_target_pairs={{0,2},{2,4},{4,6},{6,8},{8,10},{10,12},{12,14},{14,0},{1,3},{3,5},... | collective-permute-start | bytes 313352 | tf_op jit(solution)/shard_map/ppermute | solution.py:269
  4.9 8.0 %collective-permute-start.1 = (bf16[136,384]{1,0:T(8,128)(2,1)S(1)}, bf16[136,384]{1,0:T(8,128)(2,1)S(1)}, u32[]{:S(2)}, u32[]{:S(2)}) collective-permute-start(bf16[136,384]{1,0:T(8,128)(2,1)S(1)} %get-tuple-element.18.latest), channel_id=1, source_target_pairs={{0,4},{2,6},{4,8},{6,10},{8,12},{10,14},{12,0},{14,2},{1,5},{3,7},... | collective-permute-start | bytes 313352 | tf_op jit(solution)/shard_map/ppermute | solution.py:270
  6.5 6.4 %collective-permute-start.2 = (bf16[136,384]{1,0:T(8,128)(2,1)S(1)}, bf16[136,384]{1,0:T(8,128)(2,1)S(1)}, u32[]{:S(2)}, u32[]{:S(2)}) collective-permute-start(bf16[136,384]{1,0:T(8,128)(2,1)S(1)} %get-tuple-element.19.before), channel_id=1, source_target_pairs={{0,2},{2,4},{4,6},{6,8},{8,10},{10,12},{12,14},{1,3},{3,5},{5,7},{... | collective-permute-start | bytes 313352 | tf_op jit(solution)/shard_map/ppermute | solution.py:271
